TPU v7x, 512 devices: a whole 4x8x8 slice. The times are simulated.
512 devices in a mesh: row: 32 (over y_hi, z), col: 16 (over x, y_lo, core).
Axes of the slice: x: 4, y: 8 (y_hi: 4, y_lo: 2; y = y_hi * 2 + y_lo), z: 8, core: 2. Of those that a mesh axis runs over, the one named last changes fastest.
Arguments:
- anc_inverse: bfloat16 [1, 32, 256, 2, 16, 256], P(None, 'row', None, None, 'col'), may hold values from -6 to 6
- factor_one: bfloat16 [1, 32, 256, 2, 16, 256], P(None, 'row', None, None, 'col'), may hold values from -0.0625 to 0.0625
- factor_two: bfloat16 [1, 32, 256, 1, 16, 256], P(None, 'row', None, None, 'col'), may hold values from -0.0625 to 0.0625
- parent_block: bfloat16 [1, 16, 256, 256], P(None, 'col'), may hold values from -0.375 to 0.375
- diag_one: float32 [2, 16, 256, 256], P(None, 'col'), may hold values from -6 to 6
- diag_two: float32 [1, 16, 256, 256], P(None, 'col'), may hold values from -6 to 6
- pattern_one: int32 [1, 32, 2, 16], P(None, 'row', None, 'col'), may hold values from 0 to 1
- pattern_two: int32 [1, 32, 1, 16], P(None, 'row', None, 'col'), may hold values from 0 to 1, as said below
- parent: int32 [1, 16], P(None, 'col'), may hold values from 0 to 31, as said below
Outputs:
- inv_one: bfloat16 [1, 32, 256, 2, 16, 256], P(None, 'row', None, None, 'col')
- diag_inv_one: float32 [2, 16, 256, 256], P(None, 'col')
- inv_two: bfloat16 [1, 32, 256, 1, 16, 256], P(None, 'row', None, None, 'col')
- parent_inv: bfloat16 [1, 16, 256, 256], P(None, 'col')
- diag_inv_two: float32 [1, 16, 256, 256], P(None, 'col')
Inputs may be any that keep to these rules, and one draw needn't show every extreme that they name: pattern_two[J, K] is zero wherever pattern_one[J, P(K)] is zero. parent[k, c] is a level-one supernode whose index leaves remainder c when divided by 16.
All inputs are finite; a program needn't handle non-finite values.
Results may differ from a plain program's by a relative error of at most 0.007.
Values may be sent and summed in bfloat16 or wider, within the bound.
A program may use at most 64 MiB of HBM per device.

v0:
```python
import jax
import jax.numpy as jnp
from jax import lax
from jax.sharding import PartitionSpec as P


def rows_step(whole_anc, anc_rows, block):

    def add_rows(total, piece, start):
        count = piece.shape[1]
        left = whole_anc.reshape(anc_rows * block, anc_rows * count * block)
        right = piece.reshape(anc_rows * count * block, piece.shape[3] * block)
        return jnp.dot(left, right, preferred_element_type=jnp.float32)

    return add_rows


def body(
    anc_inverse,
    factor_one,
    factor_two,
    parent_block,
    diag_one,
    diag_two,
    pattern_one,
    pattern_two,
    parent,
):
    anc_rows = anc_inverse.shape[0]
    block = anc_inverse.shape[2]
    first_count = factor_one.shape[3]
    second_count = factor_two.shape[3]
    grid_rows = lax.axis_size("row")
    grid_cols = lax.axis_size("col")
    first_factor = factor_one * pattern_one.astype(jnp.bfloat16)[:, :, None, :, :, None]
    second_factor = factor_two * pattern_two.astype(jnp.bfloat16)[:, :, None, :, :, None]
    first_empty = jnp.zeros((anc_rows * block, first_count * block), jnp.float32)
    second_empty = jnp.zeros((anc_rows * block, second_count * block), jnp.float32)
    whole_anc = lax.all_gather(anc_inverse, "col", axis=4, tiled=True).reshape(
        anc_rows * block, anc_rows, grid_rows, block
    )
    add_rows = rows_step(whole_anc, anc_rows, block)
    first_total = add_rows(
        first_empty, lax.all_gather(first_factor, "row", axis=1, tiled=True), jnp.int32(0)
    )
    first_shape = (anc_rows, block, first_count, block)
    second_shape = (anc_rows, block, second_count, block)
    first_keep = pattern_one.astype(jnp.float32)
    second_keep = pattern_two.astype(jnp.float32)
    first_inv = (-first_total.reshape(first_shape) * first_keep).astype(jnp.bfloat16)
    first_cols = first_factor.reshape(first_shape)
    second_cols = second_factor.reshape(second_shape)
    diag_part = jnp.einsum(
        "ixky,ixkz->kyz", first_cols, first_inv, preferred_element_type=jnp.float32
    )
    local_parent = parent.reshape(second_count) // grid_cols
    parent_cols = jnp.take(first_inv, local_parent, axis=2)
    cross_part = jnp.einsum(
        "ixky,ixkz->kyz", parent_cols, second_cols, preferred_element_type=jnp.float32
    )
    diag_sum, cross_sum = lax.psum((diag_part, cross_part), "row")
    first_diag = diag_one.reshape(first_count, block, block) - diag_sum
    parent_diag = jnp.take(first_diag.astype(jnp.bfloat16), local_parent, axis=0)
    coupling = parent_block.reshape(second_count, block, block)
    parent_inv = (
        -(
            jnp.einsum("kyx,kxz->kyz", parent_diag, coupling, preferred_element_type=jnp.float32)
            + cross_sum
        )
    ).astype(jnp.bfloat16)
    second_total = add_rows(
        second_empty, lax.all_gather(second_factor, "row", axis=1, tiled=True), jnp.int32(0)
    )
    side = jnp.einsum("ixky,kyz->ixkz", parent_cols, coupling, preferred_element_type=jnp.float32)
    second_inv = (-(second_total.reshape(second_shape) + side) * second_keep).astype(jnp.bfloat16)
    child_part = jnp.einsum(
        "ixky,ixkz->kyz", second_cols, second_inv, preferred_element_type=jnp.float32
    )
    child_sum = lax.psum(child_part.astype(jnp.bfloat16), "row").astype(jnp.float32)
    parent_terms = jnp.einsum(
        "kxy,kxz->kyz", coupling, parent_inv, preferred_element_type=jnp.float32
    )
    second_diag = diag_two.reshape(second_count, block, block) - (child_sum + parent_terms)
    return (
        first_inv.reshape(factor_one.shape),
        first_diag.reshape(diag_one.shape),
        second_inv.reshape(factor_two.shape),
        parent_inv.reshape(parent_block.shape),
        second_diag.reshape(diag_two.shape),
    )


def solution(mesh):
    placed = (
        P(None, "row", None, None, "col", None),
        P(None, "row", None, None, "col", None),
        P(None, "row", None, None, "col", None),
        P(None, "col", None, None),
        P(None, "col", None, None),
        P(None, "col", None, None),
        P(None, "row", None, "col"),
        P(None, "row", None, "col"),
        P(None, "col"),
    )
    return jax.shard_map(
        body,
        mesh=mesh,
        in_specs=placed,
        out_specs=(
            P(None, "row", None, None, "col", None),
            P(None, "col", None, None),
            P(None, "row", None, None, "col", None),
            P(None, "col", None, None),
            P(None, "col", None, None),
        ),
        check_vma=False,
    )
```

profile of v0, /device:TPU:40, one launch (start us, length us, event | category | flops | bytes accessed | tf_op | source)
XLA Modules:
  0.0 917.3 jit_solution(8874706373367763510)
XLA Ops:
  7.2 0.0 all-gather.4.cloned.1.call-start
  7.2 0.7 convert_bitcast_fusion
  8.0 1.7 copy_multiply_fusion
  9.7 0.0 all-gather.4.cloned.1.call-update
  9.7 0.0 all-gather.6.cloned.1.call-start
  9.8 1.8 copy.41
  11.6 0.0 all-gather.6.cloned.1.call-update
  11.6 0.0 all-gather.8.cloned.1.call-start
  12.3 1.6 bitcast_multiply_fusion
  13.9 0.0 all-reduce.6.cloned.1.call-start
  14.6 0.6 dynamic-slice.9
  15.2 138.5 %all-gather.4.cloned.1.call-done = bf16[1,32,256,2,1,256]{5,2,4,3,0,1:T(8,128)(2,1)} async-done(((bf16[1,1,256,2,1,256]{5,2,4,3,0,1:T(8,128)(2,1)}), bf16[1,32,256,2,1,256]{5,2,4,3,0,1:T(8,128)(2,1)}) %all-gather.4.cloned.1.call-update) | async-done | bytes 8388624 | tf_op jit(solution)/shard_map/all_gather | solution.py:44
  153.7 14.6 %copy.40 = bf16[1,32,256,2,1,256]{2,1,5,3,4,0:T(8,128)(2,1)} copy(bf16[1,32,256,2,1,256]{5,2,4,3,0,1:T(8,128)(2,1)} %all-gather.4.cloned.1.call-done) | data formatting | bytes 16777216 | tf_op jit(solution)/shard_map/all_gather | solution.py:44
  168.4 16.5 %copy.53 = bf16[64,8,32,256]{3,1,2,0:T(8,128)(2,1)} copy(bf16[64,8,32,256]{3,2,1,0:T(8,128)(2,1)} %bitcast.112) | data formatting | bytes 16777216
  184.8 12.1 %all-gather.6.cloned.1.call-done = bf16[1,1,256,2,16,256]{2,5,4,3,1,0:T(8,128)(2,1)} async-done(((bf16[1,1,256,2,1,256]{2,5,4,3,1,0:T(8,128)(2,1)}), bf16[1,1,256,2,16,256]{2,5,4,3,1,0:T(8,128)(2,1)}) %all-gather.6.cloned.1.call-update) | async-done | bytes 4194320 | tf_op jit(solution)/shard_map/all_gather | solution.py:39
  196.9 7.2 convolution_negate_fusion
  204.1 0.2 copy.43
  204.3 1.5 convolution_bitcast_fusion.1
  205.8 1.1 fusion.11
  207.0 0.0 all-reduce.4.cloned.1.call-start
  207.0 94.3 %all-gather.8.cloned.1.call-done = bf16[1,32,256,1,1,256]{5,2,4,3,0,1:T(8,128)(2,1)} async-done(((bf16[1,1,256,1,1,256]{5,2,4,3,0,1:T(8,128)(2,1)}), bf16[1,32,256,1,1,256]{5,2,4,3,0,1:T(8,128)(2,1)}) %all-gather.8.cloned.1.call-update) | async-done | bytes 4194320 | tf_op jit(solution)/shard_map/all_gather | solution.py:72
  301.3 4.8 convolution_bitcast_fusion.4
  306.1 0.2 copy.42
  306.4 0.9 fusion.9
  307.2 0.8 copy.49
  308.0 0.9 fusion.10
  308.9 0.9 multiply_convert_fusion.1
  309.9 309.2 %all-reduce.6.cloned.1.call-done = (f32[2,256,256]{2,1,0:T(8,128)}, f32[1,256,256]{2,1,0:T(8,128)}) async-done(((f32[2,256,256]{2,1,0:T(8,128)}, f32[1,256,256]{2,1,0:T(8,128)}), (f32[2,256,256]{2,1,0:T(8,128)}, f32[1,256,256]{2,1,0:T(8,128)})) %all-reduce.6.cloned.1.call-update) | async-done | bytes 786448 | tf_op jit(solution)/shard_map/psum | solution.py:61
  619.1 1.1 bitcast_subtract_fusion
  620.2 1.3 fusion.8
  621.6 287.4 %all-reduce.4.cloned.1.call-done = bf16[1,256,256]{2,1,0:T(8,128)(2,1)} async-done(((bf16[1,256,256]{2,1,0:T(8,128)(2,1)}), bf16[1,256,256]{2,1,0:T(8,128)(2,1)}) %all-reduce.4.cloned.1.call-update) | async-done | bytes 131088 | tf_op jit(solution)/shard_map/psum | solution.py:79
  909.0 1.8 fusion.7
  (17 shorter events, 0.1 us)
Async XLA Ops:
  7.2 299.2 %copy-start = (bf16[1,1,256,256]{3,2,1,0:T(8,128)(2,1)S(1)}, bf16[1,1,256,256]{3,2,1,0:T(8,128)(2,1)}, u32[]{:S(2)}) copy-start(bf16[1,1,256,256]{3,2,1,0:T(8,128)(2,1)} %param.12) | copy-start | bytes 393220
  7.2 146.6 %all-gather.4.cloned.1.call-start = ((), (), s32[]{:S(2)}) async-start(), calls=%async_computation | async-start | bytes 8650752 | tf_op jit(solution)/shard_map/all_gather | solution.py:44
  9.7 187.2 %all-gather.6.cloned.1.call-start = ((), (), s32[]{:S(2)}) async-start(), calls=%async_computation.1 | async-start | bytes 4456448 | tf_op jit(solution)/shard_map/all_gather | solution.py:39
  11.6 289.7 %all-gather.8.cloned.1.call-start = ((), (), s32[]{:S(2)}) async-start(), calls=%async_computation.2 | async-start | bytes 4325376 | tf_op jit(solution)/shard_map/all_gather | solution.py:72
  13.9 605.2 %all-reduce.6.cloned.1.call-start = ((), (), s32[]{:S(2)}) async-start(), calls=%async_computation.4 | async-start | bytes 1572864 | tf_op jit(solution)/shard_map/psum | solution.py:61
  196.9 7.4 copy-start.2
  196.9 8.9 copy-start.1
  207.0 702.0 %all-reduce.4.cloned.1.call-start = ((), (), s32[]{:S(2)}) async-start(), calls=%async_computation.3 | async-start | bytes 262144 | tf_op jit(solution)/shard_map/psum | solution.py:79
  301.3 317.8 %copy-start.4 = (f32[2,1,256,256]{3,2,1,0:T(8,128)S(1)}, f32[2,1,256,256]{3,2,1,0:T(8,128)}, u32[]{:S(2)}) copy-start(f32[2,1,256,256]{3,2,1,0:T(8,128)} %param.13) | copy-start | bytes 1572868
  306.1 602.9 %copy-start.6 = (f32[1,1,256,256]{3,2,1,0:T(8,128)S(1)}, f32[1,1,256,256]{3,2,1,0:T(8,128)}, u32[]{:S(2)}) copy-start(f32[1,1,256,256]{3,2,1,0:T(8,128)} %param.14) | copy-start | bytes 786436
  620.2 290.6 %copy-start.3 = (f32[2,256,256]{2,1,0:T(8,128)}, f32[2,256,256]{2,1,0:T(8,128)S(1)}, u32[]{:S(2)}) copy-start(f32[2,256,256]{2,1,0:T(8,128)S(1)} %bitcast_subtract_fusion) | copy-start | bytes 1572868
  621.5 289.3 %copy-start.5 = (bf16[1,256,256]{2,1,0:T(8,128)(2,1)}, bf16[1,256,256]{2,1,0:T(8,128)(2,1)S(1)}, u32[]{:S(2)}) copy-start(bf16[1,256,256]{2,1,0:T(8,128)(2,1)S(1)} %fusion.8) | copy-start | bytes 393220
Sparse Core Ops, SparseCore 0:
  11.8 141.9 all-gather.3
  156.4 40.4 all-gather.5
  200.7 100.6 all-gather.7
  304.7 314.3 all-reduce.5
  622.7 286.2 all-reduce.3
where the time goes:
time: 918 us; the launch traced here: 917 us
  waiting for transfers between devices  842 us (92%)
  local copies, waits for them, and re-layouts  34.7 us (4%)
  matrix products  19.5 us (2%)
  between operations  15.2 us (2%)
    psum x1, waiting for transfers between devices, body(): diag_sum, cross_sum = lax.psum((diag_part, cross_part), 'row')  309 us
    psum x1, waiting for transfers between devices, body(): lax.psum(child_part.astype(jnp.bfloat16), 'row').astype(jnp.float32)  287 us
    all_gather x1, waiting for transfers between devices, body(): lax.all_gather(first_factor, 'row', axis=1, tiled=True)  139 us
    all_gather x1, waiting for transfers between devices, body(): lax.all_gather(second_factor, 'row', axis=1, tiled=True)  94.3 us
    unnamed x17, local copies, waits for them, and re-layouts  19.1 us
  transfers between devices with their start and end apart: 5, of which 5 were waited for; matrix products, arithmetic and copies ran while one was open for 6% of the time, Pallas kernels for 0%

commit v1 on v0

--- a/solution.py
+++ b/solution.py
@@ -76,7 +76,9 @@
     child_part = jnp.einsum(
         "ixky,ixkz->kyz", second_cols, second_inv, preferred_element_type=jnp.float32
     )
-    child_sum = lax.psum(child_part.astype(jnp.bfloat16), "row").astype(jnp.float32)
+    child_sum = jnp.sum(lax.all_gather(child_part.astype(jnp.bfloat16), "row"), axis=0).astype(
+        jnp.float32
+    )
     parent_terms = jnp.einsum(
         "kxy,kxz->kyz", coupling, parent_inv, preferred_element_type=jnp.float32
     )

time: 918 us -> 735 us (0.80)
  the two profiles are of different devices: /device:TPU:40 before, /device:TPU:2 now
where the time goes in v1:
time: 735 us
  waiting for transfers between devices  657 us (89%)
  local copies, waits for them, and re-layouts  35.8 us (5%)
  matrix products  17.9 us (2%)
  between operations  15.2 us (2%)
  other arithmetic  8.89 us (1%)
    psum x1, waiting for transfers between devices, body(): diag_sum, cross_sum = lax.psum((diag_part, cross_part), 'row')  309 us
    all_gather x1, waiting for transfers between devices, body(): lax.all_gather(first_factor, 'row', axis=1, tiled=True)  140 us
    all_gather x1, waiting for transfers between devices, body(): lax.all_gather(child_part.astype(jnp.bfloat16), 'row')  99.8 us
    all_gather x1, waiting for transfers between devices, body(): lax.all_gather(second_factor, 'row', axis=1, tiled=True)  96.9 us
    unnamed x19, local copies, waits for them, and re-layouts  20.1 us
  transfers between devices with their start and end apart: 5, of which 5 were waited for; matrix products, arithmetic and copies ran while one was open for 8% of the time, Pallas kernels for 0%

profile of v1, /device:TPU:2, one launch (start us, length us, event | category | flops | bytes accessed | tf_op | source)
XLA Modules:
  0.0 734.7 jit_solution(6466807105872588584)
XLA Ops:
  7.2 0.7 convert_bitcast_fusion
  8.0 1.7 copy_multiply_fusion
  9.7 0.0 all-gather.8.cloned.1.call-start
  9.8 1.8 copy.45
  12.3 1.6 bitcast_multiply_fusion
  13.9 0.0 all-reduce.3.cloned.1.call-start
  14.6 0.6 dynamic-slice.9
  15.2 140.2 %all-gather.6.cloned.1.call-done = bf16[1,32,256,2,1,256]{5,2,4,3,0,1:T(8,128)(2,1)} async-done(((bf16[1,1,256,2,1,256]{5,2,4,3,0,1:T(8,128)(2,1)}), bf16[1,32,256,2,1,256]{5,2,4,3,0,1:T(8,128)(2,1)}) %all-gather.6.cloned.1.call-update) | async-done | bytes 8388624 | tf_op jit(solution)/shard_map/all_gather | solution.py:44
  155.5 14.6 %copy.44 = bf16[1,32,256,2,1,256]{2,1,5,3,4,0:T(8,128)(2,1)} copy(bf16[1,32,256,2,1,256]{5,2,4,3,0,1:T(8,128)(2,1)} %all-gather.6.cloned.1.call-done) | data formatting | bytes 16777216 | tf_op jit(solution)/shard_map/all_gather | solution.py:44
  170.1 16.5 %copy.58 = bf16[64,8,32,256]{3,1,2,0:T(8,128)(2,1)} copy(bf16[64,8,32,256]{3,2,1,0:T(8,128)(2,1)} %bitcast.109) | data formatting | bytes 16777216
  186.6 10.4 %all-gather.8.cloned.1.call-done = bf16[1,1,256,2,16,256]{2,5,4,3,1,0:T(8,128)(2,1)} async-done(((bf16[1,1,256,2,1,256]{2,5,4,3,1,0:T(8,128)(2,1)}), bf16[1,1,256,2,16,256]{2,5,4,3,1,0:T(8,128)(2,1)}) %all-gather.8.cloned.1.call-update) | async-done | bytes 4194320 | tf_op jit(solution)/shard_map/all_gather | solution.py:39
  197.0 7.2 convolution_negate_fusion
  204.2 0.2 copy.47
  204.4 1.5 convolution_bitcast_fusion.1
  205.9 1.1 fusion.10
  207.0 0.0 all-gather.12.cloned.1.call-start
  207.1 96.9 %all-gather.10.cloned.1.call-done = bf16[1,32,256,1,1,256]{5,2,4,3,0,1:T(8,128)(2,1)} async-done(((bf16[1,1,256,1,1,256]{5,2,4,3,0,1:T(8,128)(2,1)}), bf16[1,32,256,1,1,256]{5,2,4,3,0,1:T(8,128)(2,1)}) %all-gather.10.cloned.1.call-update) | async-done | bytes 4194320 | tf_op jit(solution)/shard_map/all_gather | solution.py:72
  303.9 4.8 convolution_bitcast_fusion.4
  308.7 0.9 fusion.9
  309.7 0.9 convolution_convert_fusion
  310.6 0.1 copy.51
  310.7 0.2 copy.46
  311.0 0.8 copy.54
  311.7 0.9 multiply_convert_fusion.1
  312.7 309.2 %all-reduce.3.cloned.1.call-done = (f32[2,256,256]{2,1,0:T(8,128)}, f32[1,256,256]{2,1,0:T(8,128)}) async-done(((f32[2,256,256]{2,1,0:T(8,128)}, f32[1,256,256]{2,1,0:T(8,128)}), (f32[2,256,256]{2,1,0:T(8,128)}, f32[1,256,256]{2,1,0:T(8,128)})) %all-reduce.3.cloned.1.call-update) | async-done | bytes 786448 | tf_op jit(solution)/shard_map/psum | solution.py:61
  621.9 1.1 bitcast_subtract_fusion
  623.0 1.3 fusion.8
  624.4 99.8 %all-gather.12.cloned.1.call-done = bf16[8192,256]{1,0:T(8,128)(2,1)} async-done(((bf16[256,256]{1,0:T(8,128)(2,1)}), bf16[8192,256]{1,0:T(8,128)(2,1)}) %all-gather.12.cloned.1.call-update) | async-done | bytes 4194320 | tf_op jit(solution)/shard_map/all_gather | solution.py:79
  724.2 2.8 reduce.2
  727.0 0.1 copy.52
  727.1 0.2 fusion.2
  727.3 0.8 copy.55
  (21 shorter events, 0.2 us)
Async XLA Ops:
  7.2 301.6 %copy-start = (bf16[1,1,256,256]{3,2,1,0:T(8,128)(2,1)S(1)}, bf16[1,1,256,256]{3,2,1,0:T(8,128)(2,1)}, u32[]{:S(2)}) copy-start(bf16[1,1,256,256]{3,2,1,0:T(8,128)(2,1)} %param.12) | copy-start | bytes 393220
  7.2 148.3 %all-gather.6.cloned.1.call-start = ((), (), s32[]{:S(2)}) async-start(), calls=%async_computation | async-start | bytes 8650752 | tf_op jit(solution)/shard_map/all_gather | solution.py:44
  9.7 187.3 %all-gather.8.cloned.1.call-start = ((), (), s32[]{:S(2)}) async-start(), calls=%async_computation.1 | async-start | bytes 4456448 | tf_op jit(solution)/shard_map/all_gather | solution.py:39
  11.6 292.3 %all-gather.10.cloned.1.call-start = ((), (), s32[]{:S(2)}) async-start(), calls=%async_computation.2 | async-start | bytes 4325376 | tf_op jit(solution)/shard_map/all_gather | solution.py:72
  13.9 608.0 %all-reduce.3.cloned.1.call-start = ((), (), s32[]{:S(2)}) async-start(), calls=%async_computation.4 | async-start | bytes 1572864 | tf_op jit(solution)/shard_map/psum | solution.py:61
  197.0 7.4 %copy-start.2 = (bf16[1,1,256,1,1,256]{5,2,4,3,0,1:T(8,128)(2,1)S(1)}, bf16[1,1,256,1,1,256]{5,2,4,3,0,1:T(8,128)(2,1)}, u32[]{:S(2)}) copy-start(bf16[1,1,256,1,1,256]{5,2,4,3,0,1:T(8,128)(2,1)} %bitcast_multiply_fusion) | copy-start | bytes 393220
  197.0 8.9 %copy-start.1 = (bf16[1,1,256,2,1,256]{5,2,4,3,0,1:T(8,128)(2,1)S(1)}, bf16[1,1,256,2,1,256]{5,2,4,3,0,1:T(8,128)(2,1)}, u32[]{:S(2)}) copy-start(bf16[1,1,256,2,1,256]{5,2,4,3,0,1:T(8,128)(2,1)} %copy_multiply_fusion) | copy-start | bytes 786436
  207.0 517.2 %all-gather.12.cloned.1.call-start = ((), (), s32[]{:S(2)}) async-start(), calls=%async_computation.3 | async-start | bytes 4325376 | tf_op jit(solution)/shard_map/all_gather | solution.py:79
  303.9 6.7 copy-start.6
  308.7 313.2 %copy-start.4 = (f32[2,1,256,256]{3,2,1,0:T(8,128)S(1)}, f32[2,1,256,256]{3,2,1,0:T(8,128)}, u32[]{:S(2)}) copy-start(f32[2,1,256,256]{3,2,1,0:T(8,128)} %param.13) | copy-start | bytes 1572868
  623.0 105.2 %copy-start.3 = (f32[2,256,256]{2,1,0:T(8,128)}, f32[2,256,256]{2,1,0:T(8,128)S(1)}, u32[]{:S(2)}) copy-start(f32[2,256,256]{2,1,0:T(8,128)S(1)} %bitcast_subtract_fusion) | copy-start | bytes 1572868
  624.4 103.8 %copy-start.5 = (bf16[1,256,256]{2,1,0:T(8,128)(2,1)}, bf16[1,256,256]{2,1,0:T(8,128)(2,1)S(1)}, u32[]{:S(2)}) copy-start(bf16[1,256,256]{2,1,0:T(8,128)(2,1)S(1)} %fusion.8) | copy-start | bytes 393220
Sparse Core Ops, SparseCore 0:
  11.8 143.6 all-gather.5
  158.1 38.8 all-gather.7
  200.7 103.1 all-gather.9
  307.3 314.5 all-reduce.2
  626.0 98.1 all-gather.11
